TPU v7x, 32 devices: a whole 2x2x4 slice. The times are simulated.
32 devices in a mesh: rows: 16 (over z, y, x), rep: 2 (over core).
Axes of the slice: x: 2, y: 2, z: 4, core: 2. Of those that a mesh axis runs over, the one named last changes fastest.
Arguments:
- features: bfloat16 [4096, 128], P(('rows', 'rep')), may hold values from -6 to 6
- tile_counts: int32 [4096, 128, 128], P(('rows', 'rep')), may hold values from 0 to 3, as said below
- tile_row: int32 [4096], P(('rows', 'rep')), may hold values from 0 to 1
- tile_col: int32 [4096], P(('rows', 'rep')), may hold values from 0 to 31, as said below
- label_ids: int32 [2048], P(('rows', 'rep')), may hold values from 0 to 4095, as said below
- cotangent: bfloat16 [4096, 256], P(('rows', 'rep')), may hold values from -6 to 6
- self_weight: bfloat16 [128, 256], replicated, may hold values from -0.5 to 0.5
- neigh_weight: bfloat16 [128, 256], replicated, may hold values from -0.5 to 0.5
Outputs:
- activation: bfloat16 [4096, 256], P(('rows', 'rep'))
- grad_features: float32 [4096, 128], P(('rows', 'rep'))
- grad_self: float32 [128, 256], replicated
- grad_neigh: float32 [128, 256], replicated
Inputs may be any that keep to these rules, and one draw needn't show every extreme that they name: `tile_counts`: edge counts of one tile; most entries are zero. `tile_col`: every tile held by a device of rep index c names a column block of the feature rows of some device of rep index c. On each device, at most 16 tiles name column blocks held by devices of one rows index, and exactly 16 do for some rows index. `label_ids`: the ids of one device's 64 labels are distinct and lie among that device's own feature rows.
All inputs are finite; a program needn't handle non-finite values.
Results may differ from a plain program's by a relative error of at most 0.0053.
Values may be sent and summed in bfloat16 or wider, within the bound.
A program may use at most 128 MiB of HBM per device.

v0:
```python
import functools

import jax
import jax.numpy as jnp
from jax import lax
from jax.experimental import pallas as pl
from jax.experimental.pallas import tpu as pltpu
from jax.sharding import PartitionSpec as P

edge_moment = 14.0 / 96.0
MESH = pl.DeviceIdType.MESH
NT = (((1,), (1,)), ((), ()))
TN = (((0,), (0,)), ((), ()))


def dot(a, b, dims=(((1,), (0,)), ((), ()))):
    return lax.dot_general(a, b, dims, preferred_element_type=jnp.float32)


def table_kernel(row_s, col_s, table, filled, *, rep_count, cap):
    tiles = row_s.shape[0]
    group = 8 if tiles % 8 == 0 else 1

    @pl.loop(0, filled.shape[0])
    def _(j):
        filled[j] = 0
        for k in range(cap):
            table[j * cap + k] = 2 * tiles

    @pl.loop(0, tiles // group)
    def _(g):
        for u in range(group):
            t = g * group + u
            owner = col_s[t] // rep_count
            have = filled[owner]
            table[owner * cap + have] = 2 * t + row_s[t]
            filled[owner] = have + 1


def slot_table(tile_row, tile_col, n, rep_count, cap):
    return pl.pallas_call(
        functools.partial(table_kernel, rep_count=rep_count, cap=cap),
        out_shape=jax.ShapeDtypeStruct((n * cap,), jnp.int32),
        grid_spec=pltpu.PrefetchScalarGridSpec(
            num_scalar_prefetch=2,
            grid=(),
            in_specs=[],
            out_specs=pl.BlockSpec(memory_space=pltpu.SMEM),
            scratch_shapes=[pltpu.SMEM((n,), jnp.int32)],
        ),
        compiler_params=pltpu.CompilerParams(vmem_limit_bytes=60 * 1024 * 1024),
        cost_estimate=pl.CostEstimate(flops=1 << 33, bytes_accessed=1 << 24, transcendentals=0),
        name="slot_table",
    )(tile_row, tile_col)


def finish_kernel(*refs):
    count = len(refs) // 2
    sems = refs[-1]
    copies = [
        pltpu.make_async_copy(refs[k], refs[count + k], sems.at[k]) for k in range(count)
    ]
    for copy in copies:
        copy.start()
    for copy in copies:
        copy.wait()


def finish(arrays):
    return pl.pallas_call(
        finish_kernel,
        out_shape=tuple(jax.ShapeDtypeStruct(a.shape, a.dtype) for a in arrays),
        in_specs=[pl.BlockSpec(memory_space=pltpu.VMEM)] * len(arrays),
        out_specs=tuple(pl.BlockSpec(memory_space=pl.ANY) for _ in arrays),
        scratch_shapes=[pltpu.SemaphoreType.DMA((len(arrays),))],
        compiler_params=pltpu.CompilerParams(vmem_limit_bytes=4 * 1024 * 1024),
        name="finish",
    )(*arrays)


def layer_kernel(
    n, zs, ps, cap, scale, grad_scale,
    table, counts, feat, ids, cot, ws, wn,
    act_out, grad_out, self_out, neigh_out,
    buf, adj, gath, part, part_in, bt, tt, r1, s2, r2, wpart, win, wc, wr1, wz, wo,
    ag_s, ag_r, pair_s, pair_r, r1_s, r1_r, r2_s, r2_r, w1_s, w1_r, wz_s, wz_r, wo_s, wo_r, tile_s,
):
    me = lax.axis_index("rows")
    rep = lax.axis_index("rep")
    other = 1 - rep
    mz, mp = me // ps, me % ps
    half, f_in = feat.shape

    def zrow(d):
        return (mz + d) % zs

    def prow(d):
        return (mp + d) % ps

    def send(src, dst, ssem, rsem, row, core):
        copy = pltpu.make_async_remote_copy(
            src_ref=src, dst_ref=dst, send_sem=ssem, recv_sem=rsem,
            device_id=(row, core), device_id_type=MESH,
        )
        copy.start()
        sent.append(copy)
        return copy

    def arrived(dst, ssem, rsem):
        pltpu.make_async_remote_copy(
            src_ref=dst, dst_ref=dst, send_sem=ssem, recv_sem=rsem,
            device_id=(me, other), device_id_type=MESH,
        ).wait_recv()

    sent = []
    tiles = counts.shape[0]
    parts = tile_s.shape[0]
    size = tiles // parts
    fetches = []
    for c in range(parts):
        fetches.append(
            pltpu.make_async_copy(
                counts.at[pl.ds(c * size, size)], buf.at[pl.ds(c * size, size)], tile_s.at[c]
            )
        )
        fetches[-1].start()
    barrier = pltpu.get_barrier_semaphore()
    for d in range(1, zs):
        pl.semaphore_signal(barrier, inc=1, device_id=(zrow(d) * ps + mp, rep), device_id_type=MESH)
    for d in range(1, ps):
        for core in (rep, other):
            pl.semaphore_signal(
                barrier, inc=1, device_id=(mz * ps + prow(d), core), device_id_type=MESH
            )
    pl.semaphore_signal(barrier, inc=1, device_id=(me, other), device_id_type=MESH)
    pl.semaphore_wait(barrier, zs + 2 * (ps - 1))

    for d in range(1, zs):
        send(feat, gath.at[me], ag_s.at[d - 1], ag_r.at[me], zrow(d) * ps + mp, rep)
    for d in range(1, ps):
        send(feat, gath.at[me], ag_s.at[zs - 2 + d], ag_r.at[me], mz * ps + prow(d), rep)
    gath[me] = feat[...]
    first = dot(feat[...], ws[...])
    near = lax.broadcasted_iota(jnp.int32, (half, ids.shape[1]), 0)
    hits = (near == ids[...] - (me * 2 + rep) * half).astype(jnp.float32)
    masked = cot[...].astype(jnp.float32) * jnp.max(hits, axis=1, keepdims=True)
    buf[tiles] = jnp.zeros((half, half), jnp.int32)

    def pass_on(e):
        src = zrow(zs - e) * ps + mp
        arrived(gath.at[src], ag_s.at[0], ag_r.at[src])
        for d in range(1, ps):
            send(
                gath.at[src], gath.at[src], ag_s.at[zs - 2 + e * (ps - 1) + d], ag_r.at[src],
                mz * ps + prow(d), rep,
            )

    def build_plane(zt):
        @pl.loop(0, ps)
        def _(q):
            j = zt * ps + q
            both = jnp.zeros((half, half), jnp.int32)
            low = both
            for k in range(cap):
                entry = table[j * cap + k]
                tile = buf[entry // 2]
                both = both + tile
                low = low + tile * (entry % 2)
            cols = pl.ds(pl.multiple_of(j * half, half), half)
            adj[:half, cols] = (both - low).astype(jnp.float32).astype(jnp.bfloat16)
            adj[half:, cols] = low.astype(jnp.float32).astype(jnp.bfloat16)

    pass_on(1)
    for fetch in fetches:
        fetch.wait()
    for e in range(zs):
        build_plane(zrow(zs - e))
        if 2 <= e + 2 < zs:
            pass_on(e + 2)

    span = ps * half

    def plane_cols(zt):
        return adj[:, pl.ds(pl.multiple_of(zt * span, span), span)]

    total = jnp.zeros((2 * half, f_in), jnp.float32)
    for e in range(zs):
        zt = zrow(zs - e)
        for d in range(1, ps):
            src = zt * ps + prow(ps - d)
            arrived(gath.at[src], ag_s.at[0], ag_r.at[src])
        total = total + dot(plane_cols(zt), gath[pl.ds(zt * ps, ps)].reshape(span, f_in))
    part[...] = total.reshape(2, half, f_in)
    send(part.at[other], part_in, pair_s.at[0], pair_r.at[0], me, other)
    arrived(part_in, pair_s.at[0], pair_r.at[0])
    neighbour = (scale * (part[rep] + part_in[...])).astype(jnp.bfloat16)
    preact = first + dot(neighbour, wn[...])
    sigma = jax.nn.sigmoid(preact)
    act_out[...] = (preact * sigma).astype(jnp.bfloat16)
    delta = (masked * sigma * (1.0 + preact * (1.0 - sigma))).astype(jnp.bfloat16)
    bt[rep] = dot(wn[...], delta, NT).astype(jnp.bfloat16)
    send(bt.at[rep], bt.at[rep], pair_s.at[1], pair_r.at[1], me, other)
    wpart[0] = dot(feat[...], delta, TN)
    wpart[1] = dot(neighbour, delta, TN)
    send(wpart.at[other], win, pair_s.at[2], pair_r.at[2], me, other)
    own_term = dot(delta, ws[...], NT)

    arrived(bt.at[other], pair_s.at[1], pair_r.at[1])
    back = jnp.concatenate([bt[0], bt[1]], axis=1)

    def products(e):
        zt = zrow(e)
        out = dot(back, plane_cols(zt))
        for j in range(ps):
            tt[zt * ps + j] = out[:, j * half : (j + 1) * half].astype(jnp.bfloat16)
        for d in range(1, ps):
            k = zt * (ps - 1) + d - 1
            send(
                tt.at[zt * ps + prow(d)], r1.at[k], r1_s.at[(e - 1) * (ps - 1) + d - 1],
                r1_r.at[k], mz * ps + prow(d), rep,
            )

    products(1)
    arrived(win, pair_s.at[2], pair_r.at[2])
    wc[...] = (wpart[rep] + win[...]).astype(jnp.bfloat16).reshape(wc.shape)
    for d in range(1, ps):
        send(
            wc.at[prow(d)], wr1.at[d - 1], w1_s.at[d - 1], w1_r.at[d - 1], mz * ps + prow(d), rep
        )
    for e in range(2, zs + 1):
        products(e)
    shard = wc[mp].astype(jnp.float32)
    for d in range(1, ps):
        arrived(wr1.at[d - 1], w1_s.at[0], w1_r.at[d - 1])
        shard = shard + wr1[d - 1].astype(jnp.float32)
    wz[mz] = shard.astype(jnp.bfloat16)
    for d in range(1, zs):
        send(wz.at[mz], wz.at[mz], wz_s.at[d - 1], wz_r.at[mz], zrow(d) * ps + mp, rep)

    def plane_sum(zt):
        total = tt[zt * ps + mp].astype(jnp.float32)
        for d in range(1, ps):
            k = zt * (ps - 1) + d - 1
            arrived(r1.at[k], r1_s.at[0], r1_r.at[k])
            total = total + r1[k].astype(jnp.float32)
        return total

    for e in range(1, zs):
        s2[e - 1] = plane_sum(zrow(e)).astype(jnp.bfloat16)
        send(s2.at[e - 1], r2.at[e - 1], r2_s.at[e - 1], r2_r.at[e - 1], zrow(e) * ps + mp, rep)
    for d in range(1, zs):
        src = zrow(d)
        arrived(wz.at[src], wz_s.at[0], wz_r.at[src])
    shard = wz[0].astype(jnp.float32)
    for k in range(1, zs):
        shard = shard + wz[k].astype(jnp.float32)
    wo[rep, mp] = (grad_scale * shard).astype(jnp.bfloat16)
    send(wo.at[rep, mp], wo.at[rep, mp], wo_s.at[0], wo_r.at[rep, mp], me, other)
    for d in range(1, ps):
        for c, core in enumerate((rep, other)):
            send(
                wo.at[rep, mp], wo.at[rep, mp], wo_s.at[2 * d - 1 + c], wo_r.at[rep, mp],
                mz * ps + prow(d), core,
            )
    total = plane_sum(mz)
    for e in range(1, zs):
        arrived(r2.at[e - 1], r2_s.at[0], r2_r.at[e - 1])
        total = total + r2[e - 1].astype(jnp.float32)
    grad_out[...] = own_term + scale * jnp.transpose(total)
    arrived(wo.at[other, mp], wo_s.at[0], wo_r.at[other, mp])
    for d in range(1, ps):
        src = prow(d)
        for core in (rep, other):
            arrived(wo.at[core, src], wo_s.at[0], wo_r.at[core, src])
    self_out[...] = wo[0].astype(jnp.float32).reshape(self_out.shape)
    neigh_out[...] = wo[1].astype(jnp.float32).reshape(neigh_out.shape)
    for copy in sent:
        copy.wait_send()


def plane_size(n, width):
    return max(d for d in range(1, n + 1) if n % d == 0 and d * d <= 2 * n and width % (8 * d) == 0)


def shards(
    features, tile_counts, tile_row, tile_col, label_ids, cotangent, self_weight, neigh_weight
):
    half, f_in = features.shape
    hid = cotangent.shape[1]
    tile_total, block, _ = tile_counts.shape
    rep_count = lax.axis_size("rep")
    n = lax.axis_size("rows")
    per_half = half // block
    row_blocks = rep_count * per_half
    scale = (edge_moment * tile_total * rep_count * block / row_blocks) ** (-0.5)
    grad_scale = float(label_ids.shape[0] * n * rep_count) ** (-0.5)
    cap = tile_total * rep_count // n
    parts = 8 if tile_total % 8 == 0 else 1
    table = slot_table(tile_row, tile_col, n, rep_count, cap)
    ps = plane_size(n, f_in)
    zs = n // ps
    bf, f4 = jnp.bfloat16, jnp.float32
    dma = pltpu.SemaphoreType.DMA
    vmem = pl.BlockSpec(memory_space=pltpu.VMEM)
    outs = pl.pallas_call(
        functools.partial(layer_kernel, n, zs, ps, cap, scale, grad_scale),
        out_shape=(
            jax.ShapeDtypeStruct((half, hid), bf),
            jax.ShapeDtypeStruct((half, f_in), f4),
            jax.ShapeDtypeStruct((f_in, hid), f4),
            jax.ShapeDtypeStruct((f_in, hid), f4),
        ),
        in_specs=[pl.BlockSpec(memory_space=pltpu.SMEM), pl.BlockSpec(memory_space=pl.ANY)]
        + [vmem] * 5,
        out_specs=(vmem,) * 4,
        scratch_shapes=[
            pltpu.VMEM((tile_total + 1, block, block), jnp.int32),
            pltpu.VMEM((row_blocks * block, n * block), bf),
            pltpu.VMEM((n, half, f_in), bf),
            pltpu.VMEM((2, half, f_in), f4),
            pltpu.VMEM((half, f_in), f4),
            pltpu.VMEM((2, f_in, half), bf),
            pltpu.VMEM((n, f_in, half), bf),
            pltpu.VMEM((zs * (ps - 1), f_in, half), bf),
            pltpu.VMEM((zs - 1, f_in, half), bf),
            pltpu.VMEM((zs - 1, f_in, half), bf),
            pltpu.VMEM((2, f_in, hid), f4),
            pltpu.VMEM((f_in, hid), f4),
            pltpu.VMEM((ps, f_in // ps, hid), bf),
            pltpu.VMEM((ps - 1, f_in // ps, hid), bf),
            pltpu.VMEM((zs, f_in // ps, hid), bf),
            pltpu.VMEM((2, ps, f_in // ps, hid), bf),
            dma((n,)), dma((n,)), dma((3,)), dma((3,)),
            dma((zs * (ps - 1),)), dma((zs * (ps - 1),)), dma((zs - 1,)), dma((zs - 1,)),
            dma((ps - 1,)), dma((ps - 1,)), dma((zs - 1,)), dma((zs,)),
            dma((2 * ps - 1,)), dma((2, ps)), dma((parts,)),
        ],
        compiler_params=pltpu.CompilerParams(
            collective_id=0, has_side_effects=True, vmem_limit_bytes=50 * 1024 * 1024
        ),
        name="layer",
    )(table, tile_counts, features, label_ids.reshape(1, -1), cotangent, self_weight, neigh_weight)
    return finish(outs)


def solution(mesh):
    placed = (
        P(("rows", "rep"), None),
        P(("rows", "rep"), None, None),
        P(("rows", "rep")),
        P(("rows", "rep")),
        P(("rows", "rep")),
        P(("rows", "rep"), None),
        P(),
        P(),
    )
    return jax.shard_map(
        shards,
        mesh=mesh,
        in_specs=placed,
        out_specs=(P(("rows", "rep"), None), P(("rows", "rep"), None), P(), P()),
        check_vma=False,
    )
```

profile of v0, /device:TPU:0, one launch (start us, length us, event | category | flops | bytes accessed | tf_op | source)
XLA Modules:
  0.0 35.9 jit_solution(4460060294827090123)
XLA Ops:
  0.6 0.0 copy-start
  0.6 0.0 copy-start.1
  0.7 0.0 copy-start.2
  0.7 0.0 copy-start.3
  0.7 0.0 copy-start.5
  0.7 2.7 %slot_table.1.table = s32[256]{0:T(256)} custom-call(s32[128]{0:T(128)} %row_s.1, s32[128]{0:T(128)} %col_s.1), custom_call_target="tpu_custom_call" | custom-call | flops 8589934592 | bytes 16777216 | tf_op jit(solution)/shard_map/slot_table/pallas_call | solution.py:41
  3.4 0.0 copy-done
  3.4 0.0 copy-done.1
  3.4 0.0 copy-done.2
  3.4 0.0 copy-done.3
  3.4 0.0 copy-done.5
  3.4 0.0 copy-start.4
  3.4 0.7 %copy-done.4 = s32[256]{0:T(256)S(1)} copy-done((s32[256]{0:T(256)S(1)}, s32[256]{0:T(256)}, u32[]{:S(2)}) %copy-start.4) | copy-done | bytes 1048
  4.1 31.1 %layer.1 = (bf16[128,256]{1,0:T(8,128)(2,1)S(1)}, f32[128,128]{1,0:T(8,128)S(1)}, f32[128,256]{1,0:T(8,128)S(1)}, f32[128,256]{1,0:T(8,128)S(1)}) custom-call(s32[256]{0:T(256)S(1)} %copy-done.4, s32[128,128,128]{2,1,0:T(8,128)} %counts.1, bf16[128,128]{1,0:T(8,128)(2,1)S(1)} %copy-done.3, s32[1,64]{1,0:T(1,128)S(1)} %bitcast.1, ...), custom_call_target="tpu_custom_call" | custom-call | tf_op jit(solution)/shard_map/layer/pallas_call | solution.py:305
  35.2 0.8 %finish.1 = (bf16[128,256]{1,0:T(8,128)(2,1)}, f32[128,128]{1,0:T(8,128)}, f32[128,256]{1,0:T(8,128)}, f32[128,256]{1,0:T(8,128)}) custom-call(bf16[128,256]{1,0:T(8,128)(2,1)S(1)} %get-tuple-element.8.refs_0_, f32[128,128]{1,0:T(8,128)S(1)} %get-tuple-element.9.refs_1_, f32[128,256]{1,0:T(8,128)S(1)} %get-tuple-element.10.refs_2_, ...), custom_call_target="tpu_custom_call" | custom-call | tf_op jit(solution)/shard_map/finish/pallas_call | solution.py:70
Async XLA Ops:
  0.6 2.7 %copy-start = (bf16[128,256]{1,0:T(8,128)(2,1)S(1)}, bf16[128,256]{1,0:T(8,128)(2,1)}, u32[]{:S(2)}) copy-start(bf16[128,256]{1,0:T(8,128)(2,1)} %cot.1) | copy-start | bytes 196612
  0.6 2.7 %copy-start.1 = (bf16[128,256]{1,0:T(8,128)(2,1)S(1)}, bf16[128,256]{1,0:T(8,128)(2,1)}, u32[]{:S(2)}) copy-start(bf16[128,256]{1,0:T(8,128)(2,1)} %ws.1) | copy-start | bytes 196612
  0.7 2.7 %copy-start.2 = (bf16[128,256]{1,0:T(8,128)(2,1)S(1)}, bf16[128,256]{1,0:T(8,128)(2,1)}, u32[]{:S(2)}) copy-start(bf16[128,256]{1,0:T(8,128)(2,1)} %wn.1) | copy-start | bytes 196612
  0.7 2.7 %copy-start.3 = (bf16[128,128]{1,0:T(8,128)(2,1)S(1)}, bf16[128,128]{1,0:T(8,128)(2,1)}, u32[]{:S(2)}) copy-start(bf16[128,128]{1,0:T(8,128)(2,1)} %feat.1) | copy-start | bytes 98308
  0.7 2.7 %copy-start.5 = (s32[64]{0:T(128)S(1)}, s32[64]{0:T(128)}, u32[]{:S(2)}) copy-start(s32[64]{0:T(128)} %param.12) | copy-start | bytes 772
  3.4 0.7 %copy-start.4 = (s32[256]{0:T(256)S(1)}, s32[256]{0:T(256)}, u32[]{:S(2)}) copy-start(s32[256]{0:T(256)} %slot_table.1.table) | copy-start | bytes 3076
where the time goes:
time: 36.1 us; the launch traced here: 35.9 us
  Pallas kernels  34.5 us (96%)
  between operations  0.74 us (2%)
  local copies, waits for them, and re-layouts  0.7 us (2%)
    pallas_call x1, Pallas kernels, shards(): pl.pallas_call(functools.partial(layer_kernel, n, zs, ps, cap, scale, gra...  31.1 us
    pallas_call x1, Pallas kernels, slot_table(): pl.pallas_call(functools.partial(table_kernel, rep_count=rep_count, cap=c...  2.67 us
    pallas_call x1, Pallas kernels, finish(): pl.pallas_call(finish_kernel, out_shape=tuple((jax.ShapeDtypeStruct(a.sha...  0.78 us

commit v1 on v0

--- a/solution.py
+++ b/solution.py
@@ -15,43 +15,6 @@
 
 def dot(a, b, dims=(((1,), (0,)), ((), ()))):
     return lax.dot_general(a, b, dims, preferred_element_type=jnp.float32)
-
-
-def table_kernel(row_s, col_s, table, filled, *, rep_count, cap):
-    tiles = row_s.shape[0]
-    group = 8 if tiles % 8 == 0 else 1
-
-    @pl.loop(0, filled.shape[0])
-    def _(j):
-        filled[j] = 0
-        for k in range(cap):
-            table[j * cap + k] = 2 * tiles
-
-    @pl.loop(0, tiles // group)
-    def _(g):
-        for u in range(group):
-            t = g * group + u
-            owner = col_s[t] // rep_count
-            have = filled[owner]
-            table[owner * cap + have] = 2 * t + row_s[t]
-            filled[owner] = have + 1
-
-
-def slot_table(tile_row, tile_col, n, rep_count, cap):
-    return pl.pallas_call(
-        functools.partial(table_kernel, rep_count=rep_count, cap=cap),
-        out_shape=jax.ShapeDtypeStruct((n * cap,), jnp.int32),
-        grid_spec=pltpu.PrefetchScalarGridSpec(
-            num_scalar_prefetch=2,
-            grid=(),
-            in_specs=[],
-            out_specs=pl.BlockSpec(memory_space=pltpu.SMEM),
-            scratch_shapes=[pltpu.SMEM((n,), jnp.int32)],
-        ),
-        compiler_params=pltpu.CompilerParams(vmem_limit_bytes=60 * 1024 * 1024),
-        cost_estimate=pl.CostEstimate(flops=1 << 33, bytes_accessed=1 << 24, transcendentals=0),
-        name="slot_table",
-    )(tile_row, tile_col)
 
 
 def finish_kernel(*refs):
@@ -79,11 +42,11 @@
 
 
 def layer_kernel(
-    n, zs, ps, cap, scale, grad_scale,
-    table, counts, feat, ids, cot, ws, wn,
+    n, zs, ps, scale, grad_scale,
+    rows_h, cols_h, counts, feat_h, ids_h, cot_h, ws_h, wn_h,
     act_out, grad_out, self_out, neigh_out,
-    buf, adj, gath, part, part_in, bt, tt, r1, s2, r2, wpart, win, wc, wr1, wz, wo,
-    ag_s, ag_r, pair_s, pair_r, r1_s, r1_r, r2_s, r2_r, w1_s, w1_r, wz_s, wz_r, wo_s, wo_r, tile_s,
+    rows_v, cols_v, feat, ids, cot, ws, wn, pick, buf, adj, gath, part, part_in, bt, tt, r1, s2, r2, wpart, win, wc, wr1, wz, wo,
+    ag_s, ag_r, pair_s, pair_r, r1_s, r1_r, r2_s, r2_r, w1_s, w1_r, wz_s, wz_r, wo_s, wo_r, tile_s, in_s,
 ):
     me = lax.axis_index("rows")
     rep = lax.axis_index("rep")
@@ -115,15 +78,21 @@
     sent = []
     tiles = counts.shape[0]
     parts = tile_s.shape[0]
-    size = tiles // parts
-    fetches = []
+    size = half // parts
+    loads = []
+    for k, (src, dst) in enumerate((
+        (feat_h, feat), (rows_h, rows_v), (cols_h, cols_v), (ids_h, ids), (cot_h, cot),
+        (ws_h, ws), (wn_h, wn),
+    )):
+        loads.append(pltpu.make_async_copy(src, dst, in_s.at[k]))
+        loads[-1].start()
+
+    def part_copy(c):
+        span_i = pl.ds(pl.multiple_of(c * size, size), size)
+        return pltpu.make_async_copy(counts.at[:, span_i], buf.at[:, span_i], tile_s.at[c])
+
     for c in range(parts):
-        fetches.append(
-            pltpu.make_async_copy(
-                counts.at[pl.ds(c * size, size)], buf.at[pl.ds(c * size, size)], tile_s.at[c]
-            )
-        )
-        fetches[-1].start()
+        part_copy(c).start()
     barrier = pltpu.get_barrier_semaphore()
     for d in range(1, zs):
         pl.semaphore_signal(barrier, inc=1, device_id=(zrow(d) * ps + mp, rep), device_id_type=MESH)
@@ -135,16 +104,64 @@
     pl.semaphore_signal(barrier, inc=1, device_id=(me, other), device_id_type=MESH)
     pl.semaphore_wait(barrier, zs + 2 * (ps - 1))
 
+    loads[0].wait()
     for d in range(1, zs):
         send(feat, gath.at[me], ag_s.at[d - 1], ag_r.at[me], zrow(d) * ps + mp, rep)
     for d in range(1, ps):
         send(feat, gath.at[me], ag_s.at[zs - 2 + d], ag_r.at[me], mz * ps + prow(d), rep)
+    for load in loads[1:]:
+        load.wait()
+
+    wide = pick.shape[1]
+    sub = wide // tiles
+    lane = lax.broadcasted_iota(jnp.int32, (tiles, wide), 1)
+    widen = (lane // sub == lax.broadcasted_iota(jnp.int32, (tiles, wide), 0)).astype(jnp.float32)
+    both = jnp.concatenate(
+        [
+            jnp.broadcast_to(rows_v[...], (8, tiles)),
+            jnp.broadcast_to(cols_v[...] // 2, (8, tiles)),
+        ],
+        axis=0,
+    ).astype(jnp.float32).astype(jnp.bfloat16)
+    spread = dot(both, widen.astype(jnp.bfloat16)).astype(jnp.int32)
+    place = (spread[:1] * n + spread[8:9]) * sub + lane[:1] % sub
+    chunk = min(pick.shape[0], 2 * half)
+
+    def pick_rows(b):
+        at = lax.broadcasted_iota(jnp.int32, (chunk, wide), 0) + b * chunk
+        pick[pl.ds(b * chunk, chunk), :] = (at == place).astype(jnp.float32).astype(jnp.bfloat16)
+
+    def build(g):
+        lows, highs = [
+            buf[:, pl.ds(pl.multiple_of(g * size + k * sub, sub), sub), :]
+            .astype(jnp.float32).reshape(wide, half).astype(jnp.bfloat16)
+            for k in range(2)
+        ]
+        rhs = jnp.concatenate([lows, highs], axis=1)
+
+        def fill(b):
+            out = dot(pick[pl.ds(b * chunk, chunk), :], rhs)
+            for k in range(chunk // sub):
+                cell = b * (chunk // sub) + k
+                pair = out[k * sub : (k + 1) * sub]
+                adj[
+                    pl.ds(pl.multiple_of(cell // n * half + g * size, size), size),
+                    pl.ds(pl.multiple_of(cell % n * half, half), half),
+                ] = jnp.concatenate([pair[:, :half], pair[:, half:]], axis=0).astype(jnp.bfloat16)
+
+        blocks = pick.shape[0] // chunk
+        if blocks == 1:
+            fill(0)
+        else:
+            pl.loop(0, blocks)(fill)
+
+    for b in range(pick.shape[0] // chunk):
+        pick_rows(b)
     gath[me] = feat[...]
     first = dot(feat[...], ws[...])
     near = lax.broadcasted_iota(jnp.int32, (half, ids.shape[1]), 0)
     hits = (near == ids[...] - (me * 2 + rep) * half).astype(jnp.float32)
     masked = cot[...].astype(jnp.float32) * jnp.max(hits, axis=1, keepdims=True)
-    buf[tiles] = jnp.zeros((half, half), jnp.int32)
 
     def pass_on(e):
         src = zrow(zs - e) * ps + mp
@@ -155,28 +172,13 @@
                 mz * ps + prow(d), rep,
             )
 
-    def build_plane(zt):
-        @pl.loop(0, ps)
-        def _(q):
-            j = zt * ps + q
-            both = jnp.zeros((half, half), jnp.int32)
-            low = both
-            for k in range(cap):
-                entry = table[j * cap + k]
-                tile = buf[entry // 2]
-                both = both + tile
-                low = low + tile * (entry % 2)
-            cols = pl.ds(pl.multiple_of(j * half, half), half)
-            adj[:half, cols] = (both - low).astype(jnp.float32).astype(jnp.bfloat16)
-            adj[half:, cols] = low.astype(jnp.float32).astype(jnp.bfloat16)
-
-    pass_on(1)
-    for fetch in fetches:
-        fetch.wait()
-    for e in range(zs):
-        build_plane(zrow(zs - e))
-        if 2 <= e + 2 < zs:
-            pass_on(e + 2)
+    @pl.loop(0, parts)
+    def _(g):
+        part_copy(g).wait()
+        build(g)
+
+    for e in range(1, zs):
+        pass_on(e)
 
     span = ps * half
 
@@ -294,27 +296,33 @@
     row_blocks = rep_count * per_half
     scale = (edge_moment * tile_total * rep_count * block / row_blocks) ** (-0.5)
     grad_scale = float(label_ids.shape[0] * n * rep_count) ** (-0.5)
-    cap = tile_total * rep_count // n
-    parts = 8 if tile_total % 8 == 0 else 1
-    table = slot_table(tile_row, tile_col, n, rep_count, cap)
+    parts = half // 16
+    sub = 8
     ps = plane_size(n, f_in)
     zs = n // ps
     bf, f4 = jnp.bfloat16, jnp.float32
     dma = pltpu.SemaphoreType.DMA
     vmem = pl.BlockSpec(memory_space=pltpu.VMEM)
     outs = pl.pallas_call(
-        functools.partial(layer_kernel, n, zs, ps, cap, scale, grad_scale),
+        functools.partial(layer_kernel, n, zs, ps, scale, grad_scale),
         out_shape=(
             jax.ShapeDtypeStruct((half, hid), bf),
             jax.ShapeDtypeStruct((half, f_in), f4),
             jax.ShapeDtypeStruct((f_in, hid), f4),
             jax.ShapeDtypeStruct((f_in, hid), f4),
         ),
-        in_specs=[pl.BlockSpec(memory_space=pltpu.SMEM), pl.BlockSpec(memory_space=pl.ANY)]
-        + [vmem] * 5,
+        in_specs=[pl.BlockSpec(memory_space=pltpu.HBM)] * 8,
         out_specs=(vmem,) * 4,
         scratch_shapes=[
-            pltpu.VMEM((tile_total + 1, block, block), jnp.int32),
+            pltpu.VMEM((1, tile_total), jnp.int32),
+            pltpu.VMEM((1, tile_total), jnp.int32),
+            pltpu.VMEM((half, f_in), bf),
+            pltpu.VMEM((1, label_ids.shape[0]), jnp.int32),
+            pltpu.VMEM((half, hid), bf),
+            pltpu.VMEM((f_in, hid), bf),
+            pltpu.VMEM((f_in, hid), bf),
+            pltpu.VMEM((row_blocks * n * sub, tile_total * sub), bf),
+            pltpu.VMEM((tile_total, block, block), jnp.int32),
             pltpu.VMEM((row_blocks * block, n * block), bf),
             pltpu.VMEM((n, half, f_in), bf),
             pltpu.VMEM((2, half, f_in), f4),
@@ -333,13 +341,19 @@
             dma((n,)), dma((n,)), dma((3,)), dma((3,)),
             dma((zs * (ps - 1),)), dma((zs * (ps - 1),)), dma((zs - 1,)), dma((zs - 1,)),
             dma((ps - 1,)), dma((ps - 1,)), dma((zs - 1,)), dma((zs,)),
-            dma((2 * ps - 1,)), dma((2, ps)), dma((parts,)),
+            dma((2 * ps - 1,)), dma((2, ps)), dma((parts,)), dma((7,)),
         ],
         compiler_params=pltpu.CompilerParams(
             collective_id=0, has_side_effects=True, vmem_limit_bytes=50 * 1024 * 1024
         ),
         name="layer",
-    )(table, tile_counts, features, label_ids.reshape(1, -1), cotangent, self_weight, neigh_weight)
+    )(*[
+        pltpu.with_memory_space_constraint(a, pltpu.HBM)
+        for a in (
+            tile_row.reshape(1, -1), tile_col.reshape(1, -1), tile_counts, features,
+            label_ids.reshape(1, -1), cotangent, self_weight, neigh_weight,
+        )
+    ])
     return finish(outs)
 
 

time: 36.1 us -> 33.6 us (0.931)
  Pallas kernels: 34.5 us -> 32.8 us
  local copies, waits for them, and re-layouts: 0.7 us -> 0 us
    pallas_call x2 -> x1, Pallas kernels: 33.7 us -> 32 us  [shards(): pl.pallas_call(functools.partial(layer_kernel, n, zs, ps, scale, grad_sca...]
    unnamed x12 -> x0, local copies, waits for them, and re-layouts: 0.7 us -> none
where the time goes in v1:
time: 33.6 us; the launch traced here: 33.4 us
  Pallas kernels  32.8 us (98%)
  between operations  0.64 us (2%)
    pallas_call x1, Pallas kernels, shards(): pl.pallas_call(functools.partial(layer_kernel, n, zs, ps, scale, grad_sca...  32 us
    pallas_call x1, Pallas kernels, finish(): pl.pallas_call(finish_kernel, out_shape=tuple((jax.ShapeDtypeStruct(a.sha...  0.78 us

profile of v1, /device:TPU:0, one launch (start us, length us, event | category | flops | bytes accessed | tf_op | source)
XLA Modules:
  0.0 33.4 jit_solution(9638952660225509320)
XLA Ops:
  0.6 32.0 %layer.1 = (bf16[128,256]{1,0:T(8,128)(2,1)S(1)}, f32[128,128]{1,0:T(8,128)S(1)}, f32[128,256]{1,0:T(8,128)S(1)}, f32[128,256]{1,0:T(8,128)S(1)}) custom-call(s32[1,128]{1,0:T(1,128)} %bitcast.3, s32[1,128]{1,0:T(1,128)} %bitcast.4, s32[128,128,128]{2,1,0:T(8,128)} %counts.1, bf16[128,128]{1,0:T(8,128)(2,1)} %feat_h.1, s32[1,64]{1,0:T(1,128)} %bitcast.5, ...), custom_call_target="tpu_custom_call" | custom-call | tf_op jit(solution)/shard_map/layer/pallas_call | solution.py:306
  32.6 0.8 %finish.1 = (bf16[128,256]{1,0:T(8,128)(2,1)}, f32[128,128]{1,0:T(8,128)}, f32[128,256]{1,0:T(8,128)}, f32[128,256]{1,0:T(8,128)}) custom-call(bf16[128,256]{1,0:T(8,128)(2,1)S(1)} %get-tuple-element.8.refs_0_, f32[128,128]{1,0:T(8,128)S(1)} %get-tuple-element.9.refs_1_, f32[128,256]{1,0:T(8,128)S(1)} %get-tuple-element.10.refs_2_, ...), custom_call_target="tpu_custom_call" | custom-call | tf_op jit(solution)/shard_map/finish/pallas_call | solution.py:33

commit v2 on v1

--- a/solution.py
+++ b/solution.py
@@ -41,11 +41,20 @@
     )(*arrays)
 
 
+def flip(a, k):
+    out, bit = a, 1
+    while bit <= k:
+        if k & bit:
+            out = out + (1 - 2 * ((a // bit) % 2)) * bit
+        bit *= 2
+    return out
+
+
 def layer_kernel(
     n, zs, ps, scale, grad_scale,
     rows_h, cols_h, counts, feat_h, ids_h, cot_h, ws_h, wn_h,
     act_out, grad_out, self_out, neigh_out,
-    rows_v, cols_v, feat, ids, cot, ws, wn, pick, buf, adj, gath, part, part_in, bt, tt, r1, s2, r2, wpart, win, wc, wr1, wz, wo,
+    rows_v, cols_v, feat, ids, cot, ws, wn, pick, buf, adj, gath, part, part_in, bt, tt, r1, s2, r2, wpart, win, wz, wo,
     ag_s, ag_r, pair_s, pair_r, r1_s, r1_r, r2_s, r2_r, w1_s, w1_r, wz_s, wz_r, wo_s, wo_r, tile_s, in_s,
 ):
     me = lax.axis_index("rows")
@@ -54,8 +63,13 @@
     mz, mp = me // ps, me % ps
     half, f_in = feat.shape
 
-    def zrow(d):
-        return (mz + d) % zs
+    paired = zs & (zs - 1) == 0
+
+    def zto(k):
+        return flip(mz, k) if paired else (mz + k) % zs
+
+    def zfrom(k):
+        return flip(mz, k) if paired else (mz + zs - k) % zs
 
     def prow(d):
         return (mp + d) % ps
@@ -91,22 +105,22 @@
         span_i = pl.ds(pl.multiple_of(c * size, size), size)
         return pltpu.make_async_copy(counts.at[:, span_i], buf.at[:, span_i], tile_s.at[c])
 
-    for c in range(parts):
-        part_copy(c).start()
     barrier = pltpu.get_barrier_semaphore()
     for d in range(1, zs):
-        pl.semaphore_signal(barrier, inc=1, device_id=(zrow(d) * ps + mp, rep), device_id_type=MESH)
+        pl.semaphore_signal(barrier, inc=1, device_id=(zto(d) * ps + mp, rep), device_id_type=MESH)
     for d in range(1, ps):
         for core in (rep, other):
             pl.semaphore_signal(
                 barrier, inc=1, device_id=(mz * ps + prow(d), core), device_id_type=MESH
             )
     pl.semaphore_signal(barrier, inc=1, device_id=(me, other), device_id_type=MESH)
+    loads[0].wait()
+    for c in range(parts):
+        part_copy(c).start()
     pl.semaphore_wait(barrier, zs + 2 * (ps - 1))
 
-    loads[0].wait()
     for d in range(1, zs):
-        send(feat, gath.at[me], ag_s.at[d - 1], ag_r.at[me], zrow(d) * ps + mp, rep)
+        send(feat, gath.at[me], ag_s.at[d - 1], ag_r.at[me], zto(d) * ps + mp, rep)
     for d in range(1, ps):
         send(feat, gath.at[me], ag_s.at[zs - 2 + d], ag_r.at[me], mz * ps + prow(d), rep)
     for load in loads[1:]:
@@ -164,7 +178,7 @@
     masked = cot[...].astype(jnp.float32) * jnp.max(hits, axis=1, keepdims=True)
 
     def pass_on(e):
-        src = zrow(zs - e) * ps + mp
+        src = zfrom(e) * ps + mp
         arrived(gath.at[src], ag_s.at[0], ag_r.at[src])
         for d in range(1, ps):
             send(
@@ -172,13 +186,19 @@
                 mz * ps + prow(d), rep,
             )
 
-    @pl.loop(0, parts)
-    def _(g):
+    def build_next(g):
         part_copy(g).wait()
         build(g)
 
+    lead = parts // 2
+    pl.loop(0, lead)(build_next)
     for e in range(1, zs):
         pass_on(e)
+        if lead < parts:
+            build_next(lead)
+            lead += 1
+    if lead < parts:
+        pl.loop(lead, parts)(build_next)
 
     span = ps * half
 
@@ -187,7 +207,7 @@
 
     total = jnp.zeros((2 * half, f_in), jnp.float32)
     for e in range(zs):
-        zt = zrow(zs - e)
+        zt = zfrom(e)
         for d in range(1, ps):
             src = zt * ps + prow(ps - d)
             arrived(gath.at[src], ag_s.at[0], ag_r.at[src])
@@ -198,46 +218,43 @@
     neighbour = (scale * (part[rep] + part_in[...])).astype(jnp.bfloat16)
     preact = first + dot(neighbour, wn[...])
     sigma = jax.nn.sigmoid(preact)
-    act_out[...] = (preact * sigma).astype(jnp.bfloat16)
     delta = (masked * sigma * (1.0 + preact * (1.0 - sigma))).astype(jnp.bfloat16)
     bt[rep] = dot(wn[...], delta, NT).astype(jnp.bfloat16)
     send(bt.at[rep], bt.at[rep], pair_s.at[1], pair_r.at[1], me, other)
-    wpart[0] = dot(feat[...], delta, TN)
-    wpart[1] = dot(neighbour, delta, TN)
-    send(wpart.at[other], win, pair_s.at[2], pair_r.at[2], me, other)
+    wpart[0] = dot(feat[...], delta, TN).astype(jnp.bfloat16).reshape(wpart.shape[1:])
+    wpart[1] = dot(neighbour, delta, TN).astype(jnp.bfloat16).reshape(wpart.shape[1:])
+    peers = [(mp, other)] + [(prow(d), core) for d in range(1, ps) for core in (rep, other)]
+    for k, (p, core) in enumerate(peers):
+        send(
+            wpart.at[core, p], win.at[rep, mp], w1_s.at[k], w1_r.at[rep, mp], mz * ps + p, core
+        )
+    act_out[...] = (preact * sigma).astype(jnp.bfloat16)
     own_term = dot(delta, ws[...], NT)
 
     arrived(bt.at[other], pair_s.at[1], pair_r.at[1])
     back = jnp.concatenate([bt[0], bt[1]], axis=1)
 
     def products(e):
-        zt = zrow(e)
+        zt = zto(e)
         out = dot(back, plane_cols(zt))
         for j in range(ps):
             tt[zt * ps + j] = out[:, j * half : (j + 1) * half].astype(jnp.bfloat16)
         for d in range(1, ps):
             k = zt * (ps - 1) + d - 1
             send(
-                tt.at[zt * ps + prow(d)], r1.at[k], r1_s.at[(e - 1) * (ps - 1) + d - 1],
+                tt.at[zt * ps + prow(d)], r1.at[k], r1_s.at[e * (ps - 1) + d - 1],
                 r1_r.at[k], mz * ps + prow(d), rep,
             )
 
-    products(1)
-    arrived(win, pair_s.at[2], pair_r.at[2])
-    wc[...] = (wpart[rep] + win[...]).astype(jnp.bfloat16).reshape(wc.shape)
-    for d in range(1, ps):
-        send(
-            wc.at[prow(d)], wr1.at[d - 1], w1_s.at[d - 1], w1_r.at[d - 1], mz * ps + prow(d), rep
-        )
-    for e in range(2, zs + 1):
+    for e in range(zs - 1, -1, -1):
         products(e)
-    shard = wc[mp].astype(jnp.float32)
-    for d in range(1, ps):
-        arrived(wr1.at[d - 1], w1_s.at[0], w1_r.at[d - 1])
-        shard = shard + wr1[d - 1].astype(jnp.float32)
+    shard = wpart[rep, mp].astype(jnp.float32)
+    for p, core in peers:
+        arrived(win.at[core, p], w1_s.at[0], w1_r.at[core, p])
+        shard = shard + win[core, p].astype(jnp.float32)
     wz[mz] = shard.astype(jnp.bfloat16)
     for d in range(1, zs):
-        send(wz.at[mz], wz.at[mz], wz_s.at[d - 1], wz_r.at[mz], zrow(d) * ps + mp, rep)
+        send(wz.at[mz], wz.at[mz], wz_s.at[d - 1], wz_r.at[mz], zto(d) * ps + mp, rep)
 
     def plane_sum(zt):
         total = tt[zt * ps + mp].astype(jnp.float32)
@@ -247,33 +264,33 @@
             total = total + r1[k].astype(jnp.float32)
         return total
 
-    for e in range(1, zs):
-        s2[e - 1] = plane_sum(zrow(e)).astype(jnp.bfloat16)
-        send(s2.at[e - 1], r2.at[e - 1], r2_s.at[e - 1], r2_r.at[e - 1], zrow(e) * ps + mp, rep)
-    for d in range(1, zs):
-        src = zrow(d)
-        arrived(wz.at[src], wz_s.at[0], wz_r.at[src])
-    shard = wz[0].astype(jnp.float32)
-    for k in range(1, zs):
-        shard = shard + wz[k].astype(jnp.float32)
-    wo[rep, mp] = (grad_scale * shard).astype(jnp.bfloat16)
-    send(wo.at[rep, mp], wo.at[rep, mp], wo_s.at[0], wo_r.at[rep, mp], me, other)
-    for d in range(1, ps):
-        for c, core in enumerate((rep, other)):
+    def spread_weights():
+        for d in range(1, zs):
+            src = zfrom(d)
+            arrived(wz.at[src], wz_s.at[0], wz_r.at[src])
+        shard = wz[0].astype(jnp.float32)
+        for k in range(1, zs):
+            shard = shard + wz[k].astype(jnp.float32)
+        wo[rep, mp] = (grad_scale * shard).astype(jnp.bfloat16)
+        for k, (p, core) in enumerate(peers[1:] + peers[:1]):
             send(
-                wo.at[rep, mp], wo.at[rep, mp], wo_s.at[2 * d - 1 + c], wo_r.at[rep, mp],
-                mz * ps + prow(d), core,
+                wo.at[rep, mp], wo.at[rep, mp], wo_s.at[k], wo_r.at[rep, mp], mz * ps + p, core
             )
+
+    for e in range(zs - 1, 0, -1):
+        s2[e - 1] = plane_sum(zto(e)).astype(jnp.bfloat16)
+        send(s2.at[e - 1], r2.at[e - 1], r2_s.at[e - 1], r2_r.at[e - 1], zto(e) * ps + mp, rep)
+        if e == max(zs - 2, 1):
+            spread_weights()
+    if zs == 1:
+        spread_weights()
     total = plane_sum(mz)
     for e in range(1, zs):
         arrived(r2.at[e - 1], r2_s.at[0], r2_r.at[e - 1])
         total = total + r2[e - 1].astype(jnp.float32)
     grad_out[...] = own_term + scale * jnp.transpose(total)
-    arrived(wo.at[other, mp], wo_s.at[0], wo_r.at[other, mp])
-    for d in range(1, ps):
-        src = prow(d)
-        for core in (rep, other):
-            arrived(wo.at[core, src], wo_s.at[0], wo_r.at[core, src])
+    for p, core in peers:
+        arrived(wo.at[core, p], wo_s.at[0], wo_r.at[core, p])
     self_out[...] = wo[0].astype(jnp.float32).reshape(self_out.shape)
     neigh_out[...] = wo[1].astype(jnp.float32).reshape(neigh_out.shape)
     for copy in sent:
@@ -332,15 +349,13 @@
             pltpu.VMEM((zs * (ps - 1), f_in, half), bf),
             pltpu.VMEM((zs - 1, f_in, half), bf),
             pltpu.VMEM((zs - 1, f_in, half), bf),
-            pltpu.VMEM((2, f_in, hid), f4),
-            pltpu.VMEM((f_in, hid), f4),
-            pltpu.VMEM((ps, f_in // ps, hid), bf),
-            pltpu.VMEM((ps - 1, f_in // ps, hid), bf),
+            pltpu.VMEM((2, ps, f_in // ps, hid), bf),
+            pltpu.VMEM((2, ps, f_in // ps, hid), bf),
             pltpu.VMEM((zs, f_in // ps, hid), bf),
             pltpu.VMEM((2, ps, f_in // ps, hid), bf),
-            dma((n,)), dma((n,)), dma((3,)), dma((3,)),
+            dma((n,)), dma((n,)), dma((2,)), dma((2,)),
             dma((zs * (ps - 1),)), dma((zs * (ps - 1),)), dma((zs - 1,)), dma((zs - 1,)),
-            dma((ps - 1,)), dma((ps - 1,)), dma((zs - 1,)), dma((zs,)),
+            dma((2 * ps - 1,)), dma((2, ps)), dma((zs - 1,)), dma((zs,)),
             dma((2 * ps - 1,)), dma((2, ps)), dma((parts,)), dma((7,)),
         ],
         compiler_params=pltpu.CompilerParams(

time: 33.6 us -> 29.8 us (0.89)
  Pallas kernels: 32.8 us -> 29 us
    pallas_call x1, Pallas kernels: 32 us -> 28.2 us  [shards(): pl.pallas_call(functools.partial(layer_kernel, n, zs, ps, scale, grad_sca...]
where the time goes in v2:
time: 29.8 us; the launch traced here: 29.6 us
  Pallas kernels  29 us (97%)
  between operations  0.64 us (2%)
    pallas_call x1, Pallas kernels, shards(): pl.pallas_call(functools.partial(layer_kernel, n, zs, ps, scale, grad_sca...  28.2 us
    pallas_call x1, Pallas kernels, finish(): pl.pallas_call(finish_kernel, out_shape=tuple((jax.ShapeDtypeStruct(a.sha...  0.78 us

profile of v2, /device:TPU:0, one launch (start us, length us, event | category | flops | bytes accessed | tf_op | source)
XLA Modules:
  0.0 29.6 jit_solution(10645232694239889317)
XLA Ops:
  0.6 28.2 %layer.1 = (bf16[128,256]{1,0:T(8,128)(2,1)S(1)}, f32[128,128]{1,0:T(8,128)S(1)}, f32[128,256]{1,0:T(8,128)S(1)}, f32[128,256]{1,0:T(8,128)S(1)}) custom-call(s32[1,128]{1,0:T(1,128)} %bitcast.3, s32[1,128]{1,0:T(1,128)} %bitcast.4, s32[128,128,128]{2,1,0:T(8,128)} %counts.1, bf16[128,128]{1,0:T(8,128)(2,1)} %feat_h.1, s32[1,64]{1,0:T(1,128)} %bitcast.5, ...), custom_call_target="tpu_custom_call" | custom-call | tf_op jit(solution)/shard_map/layer/pallas_call | solution.py:323
  28.8 0.8 %finish.1 = (bf16[128,256]{1,0:T(8,128)(2,1)}, f32[128,128]{1,0:T(8,128)}, f32[128,256]{1,0:T(8,128)}, f32[128,256]{1,0:T(8,128)}) custom-call(bf16[128,256]{1,0:T(8,128)(2,1)S(1)} %get-tuple-element.8.refs_0_, f32[128,128]{1,0:T(8,128)S(1)} %get-tuple-element.9.refs_1_, f32[128,256]{1,0:T(8,128)S(1)} %get-tuple-element.10.refs_2_, ...), custom_call_target="tpu_custom_call" | custom-call | tf_op jit(solution)/shard_map/finish/pallas_call | solution.py:33

commit v3 on v2

--- a/solution.py
+++ b/solution.py
@@ -55,7 +55,7 @@
     rows_h, cols_h, counts, feat_h, ids_h, cot_h, ws_h, wn_h,
     act_out, grad_out, self_out, neigh_out,
     rows_v, cols_v, feat, ids, cot, ws, wn, pick, buf, adj, gath, part, part_in, bt, tt, r1, s2, r2, wpart, win, wz, wo,
-    ag_s, ag_r, pair_s, pair_r, r1_s, r1_r, r2_s, r2_r, w1_s, w1_r, wz_s, wz_r, wo_s, wo_r, tile_s, in_s,
+    send_s, ag_z, ag_r, pair_r, r1_r, late_r, tile_s, in_s,
 ):
     me = lax.axis_index("rows")
     rep = lax.axis_index("rep")
@@ -80,16 +80,19 @@
             device_id=(row, core), device_id_type=MESH,
         )
         copy.start()
-        sent.append(copy)
-        return copy
-
-    def arrived(dst, ssem, rsem):
-        pltpu.make_async_remote_copy(
-            src_ref=dst, dst_ref=dst, send_sem=ssem, recv_sem=rsem,
+
+    def whole(ref, ssem, rsem):
+        return pltpu.make_async_remote_copy(
+            src_ref=ref, dst_ref=ref, send_sem=ssem, recv_sem=rsem,
             device_id=(me, other), device_id_type=MESH,
-        ).wait_recv()
-
-    sent = []
+        )
+
+    def arrived(dst, rsem):
+        whole(dst, rsem, rsem).wait_recv()
+
+    def left(src, ssem):
+        whole(src, ssem, ssem).wait_send()
+
     tiles = counts.shape[0]
     parts = tile_s.shape[0]
     size = half // parts
@@ -114,15 +117,23 @@
                 barrier, inc=1, device_id=(mz * ps + prow(d), core), device_id_type=MESH
             )
     pl.semaphore_signal(barrier, inc=1, device_id=(me, other), device_id_type=MESH)
+    cube = range(1, ps) if zs > 1 else ()
+    for d in cube:
+        pl.semaphore_signal(
+            barrier, inc=1, device_id=(zto(1) * ps + prow(d), rep), device_id_type=MESH
+        )
     loads[0].wait()
     for c in range(parts):
         part_copy(c).start()
-    pl.semaphore_wait(barrier, zs + 2 * (ps - 1))
-
-    for d in range(1, zs):
-        send(feat, gath.at[me], ag_s.at[d - 1], ag_r.at[me], zto(d) * ps + mp, rep)
-    for d in range(1, ps):
-        send(feat, gath.at[me], ag_s.at[zs - 2 + d], ag_r.at[me], mz * ps + prow(d), rep)
+    pl.semaphore_wait(barrier, zs + 2 * (ps - 1) + len(cube))
+
+    firsts = [zto(k) * ps + mp for k in [*range(2, zs), 1] if k < zs]
+    firsts += [mz * ps + prow(d) for d in range(1, ps)]
+    firsts += [zto(1) * ps + prow(d) for d in cube]
+    relayed = max(zs - 2, 0)
+    for k, row in enumerate(firsts):
+        rsem = ag_z.at[mz] if k < relayed else ag_r.at[mz]
+        send(feat, gath.at[me], send_s.at[0], rsem, row, rep)
     for load in loads[1:]:
         load.wait()
 
@@ -179,10 +190,10 @@
 
     def pass_on(e):
         src = zfrom(e) * ps + mp
-        arrived(gath.at[src], ag_s.at[0], ag_r.at[src])
+        arrived(gath.at[src], ag_z.at[zfrom(e)])
         for d in range(1, ps):
             send(
-                gath.at[src], gath.at[src], ag_s.at[zs - 2 + e * (ps - 1) + d], ag_r.at[src],
+                gath.at[src], gath.at[src], send_s.at[0], ag_r.at[zfrom(e)],
                 mz * ps + prow(d), rep,
             )
 
@@ -192,7 +203,7 @@
 
     lead = parts // 2
     pl.loop(0, lead)(build_next)
-    for e in range(1, zs):
+    for e in range(2, zs):
         pass_on(e)
         if lead < parts:
             build_next(lead)
@@ -208,30 +219,30 @@
     total = jnp.zeros((2 * half, f_in), jnp.float32)
     for e in range(zs):
         zt = zfrom(e)
-        for d in range(1, ps):
-            src = zt * ps + prow(ps - d)
-            arrived(gath.at[src], ag_s.at[0], ag_r.at[src])
+        landing = ps if e == 1 else ps - 1
+        if landing:
+            arrived(gath.at[pl.ds(zt * ps, landing)], ag_r.at[zt])
         total = total + dot(plane_cols(zt), gath[pl.ds(zt * ps, ps)].reshape(span, f_in))
     part[...] = total.reshape(2, half, f_in)
-    send(part.at[other], part_in, pair_s.at[0], pair_r.at[0], me, other)
-    arrived(part_in, pair_s.at[0], pair_r.at[0])
+    send(part.at[other], part_in, send_s.at[1], pair_r.at[0], me, other)
+    arrived(part_in, pair_r.at[0])
     neighbour = (scale * (part[rep] + part_in[...])).astype(jnp.bfloat16)
     preact = first + dot(neighbour, wn[...])
     sigma = jax.nn.sigmoid(preact)
     delta = (masked * sigma * (1.0 + preact * (1.0 - sigma))).astype(jnp.bfloat16)
     bt[rep] = dot(wn[...], delta, NT).astype(jnp.bfloat16)
-    send(bt.at[rep], bt.at[rep], pair_s.at[1], pair_r.at[1], me, other)
+    send(bt.at[rep], bt.at[rep], send_s.at[2], pair_r.at[1], me, other)
     wpart[0] = dot(feat[...], delta, TN).astype(jnp.bfloat16).reshape(wpart.shape[1:])
     wpart[1] = dot(neighbour, delta, TN).astype(jnp.bfloat16).reshape(wpart.shape[1:])
     peers = [(mp, other)] + [(prow(d), core) for d in range(1, ps) for core in (rep, other)]
-    for k, (p, core) in enumerate(peers):
+    for p, core in peers:
         send(
-            wpart.at[core, p], win.at[rep, mp], w1_s.at[k], w1_r.at[rep, mp], mz * ps + p, core
+            wpart.at[core, p], win.at[rep * ps + mp], send_s.at[3], late_r.at[0], mz * ps + p, core
         )
     act_out[...] = (preact * sigma).astype(jnp.bfloat16)
     own_term = dot(delta, ws[...], NT)
 
-    arrived(bt.at[other], pair_s.at[1], pair_r.at[1])
+    arrived(bt.at[other], pair_r.at[1])
     back = jnp.concatenate([bt[0], bt[1]], axis=1)
 
     def products(e):
@@ -242,59 +253,67 @@
         for d in range(1, ps):
             k = zt * (ps - 1) + d - 1
             send(
-                tt.at[zt * ps + prow(d)], r1.at[k], r1_s.at[e * (ps - 1) + d - 1],
-                r1_r.at[k], mz * ps + prow(d), rep,
+                tt.at[zt * ps + prow(d)], r1.at[k], send_s.at[4],
+                r1_r.at[zt], mz * ps + prow(d), rep,
             )
 
     for e in range(zs - 1, -1, -1):
         products(e)
     shard = wpart[rep, mp].astype(jnp.float32)
+    arrived(win.at[pl.ds(0, len(peers))], late_r.at[0])
     for p, core in peers:
-        arrived(win.at[core, p], w1_s.at[0], w1_r.at[core, p])
-        shard = shard + win[core, p].astype(jnp.float32)
+        shard = shard + win[core * ps + p].astype(jnp.float32)
     wz[mz] = shard.astype(jnp.bfloat16)
     for d in range(1, zs):
-        send(wz.at[mz], wz.at[mz], wz_s.at[d - 1], wz_r.at[mz], zto(d) * ps + mp, rep)
+        send(wz.at[mz], wz.at[mz], send_s.at[5], late_r.at[1], zto(d) * ps + mp, rep)
 
     def plane_sum(zt):
         total = tt[zt * ps + mp].astype(jnp.float32)
+        if ps > 1:
+            arrived(r1.at[pl.ds(zt * (ps - 1), ps - 1)], r1_r.at[zt])
         for d in range(1, ps):
             k = zt * (ps - 1) + d - 1
-            arrived(r1.at[k], r1_s.at[0], r1_r.at[k])
             total = total + r1[k].astype(jnp.float32)
         return total
 
     def spread_weights():
-        for d in range(1, zs):
-            src = zfrom(d)
-            arrived(wz.at[src], wz_s.at[0], wz_r.at[src])
+        if zs > 1:
+            arrived(wz.at[pl.ds(0, zs - 1)], late_r.at[1])
         shard = wz[0].astype(jnp.float32)
         for k in range(1, zs):
             shard = shard + wz[k].astype(jnp.float32)
-        wo[rep, mp] = (grad_scale * shard).astype(jnp.bfloat16)
-        for k, (p, core) in enumerate(peers[1:] + peers[:1]):
-            send(
-                wo.at[rep, mp], wo.at[rep, mp], wo_s.at[k], wo_r.at[rep, mp], mz * ps + p, core
-            )
+        mine = rep * ps + mp
+        wo[mine] = (grad_scale * shard).astype(jnp.bfloat16)
+        for p, core in peers[1:] + peers[:1]:
+            send(wo.at[mine], wo.at[mine], send_s.at[6], late_r.at[2], mz * ps + p, core)
 
     for e in range(zs - 1, 0, -1):
         s2[e - 1] = plane_sum(zto(e)).astype(jnp.bfloat16)
-        send(s2.at[e - 1], r2.at[e - 1], r2_s.at[e - 1], r2_r.at[e - 1], zto(e) * ps + mp, rep)
+        send(s2.at[e - 1], r2.at[e - 1], send_s.at[7], late_r.at[3], zto(e) * ps + mp, rep)
         if e == max(zs - 2, 1):
             spread_weights()
     if zs == 1:
         spread_weights()
     total = plane_sum(mz)
+    if zs > 1:
+        arrived(r2, late_r.at[3])
     for e in range(1, zs):
-        arrived(r2.at[e - 1], r2_s.at[0], r2_r.at[e - 1])
         total = total + r2[e - 1].astype(jnp.float32)
     grad_out[...] = own_term + scale * jnp.transpose(total)
-    for p, core in peers:
-        arrived(wo.at[core, p], wo_s.at[0], wo_r.at[core, p])
-    self_out[...] = wo[0].astype(jnp.float32).reshape(self_out.shape)
-    neigh_out[...] = wo[1].astype(jnp.float32).reshape(neigh_out.shape)
-    for copy in sent:
-        copy.wait_send()
+    arrived(wo.at[pl.ds(0, len(peers))], late_r.at[2])
+    self_out[...] = wo[:ps].astype(jnp.float32).reshape(self_out.shape)
+    neigh_out[...] = wo[ps:].astype(jnp.float32).reshape(neigh_out.shape)
+    if n > 1:
+        left(gath.at[pl.ds(0, n - 1)], send_s.at[0])
+    left(part_in, send_s.at[1])
+    left(bt.at[rep], send_s.at[2])
+    left(win.at[pl.ds(0, len(peers))], send_s.at[3])
+    if ps > 1:
+        left(r1, send_s.at[4])
+    if zs > 1:
+        left(wz.at[pl.ds(0, zs - 1)], send_s.at[5])
+        left(r2, send_s.at[7])
+    left(wo.at[pl.ds(0, len(peers))], send_s.at[6])
 
 
 def plane_size(n, width):
@@ -350,13 +369,11 @@
             pltpu.VMEM((zs - 1, f_in, half), bf),
             pltpu.VMEM((zs - 1, f_in, half), bf),
             pltpu.VMEM((2, ps, f_in // ps, hid), bf),
-            pltpu.VMEM((2, ps, f_in // ps, hid), bf),
+            pltpu.VMEM((2 * ps, f_in // ps, hid), bf),
             pltpu.VMEM((zs, f_in // ps, hid), bf),
-            pltpu.VMEM((2, ps, f_in // ps, hid), bf),
-            dma((n,)), dma((n,)), dma((2,)), dma((2,)),
-            dma((zs * (ps - 1),)), dma((zs * (ps - 1),)), dma((zs - 1,)), dma((zs - 1,)),
-            dma((2 * ps - 1,)), dma((2, ps)), dma((zs - 1,)), dma((zs,)),
-            dma((2 * ps - 1,)), dma((2, ps)), dma((parts,)), dma((7,)),
+            pltpu.VMEM((2 * ps, f_in // ps, hid), bf),
+            dma((8,)), dma((zs,)), dma((zs,)), dma((2,)), dma((zs,)), dma((4,)), dma((parts,)),
+            dma((7,)),
         ],
         compiler_params=pltpu.CompilerParams(
             collective_id=0, has_side_effects=True, vmem_limit_bytes=50 * 1024 * 1024

time: 29.8 us -> 29.1 us (0.977)
  Pallas kernels: 29 us -> 28.3 us
    pallas_call x1, Pallas kernels: 28.2 us -> 27.5 us  [shards(): pl.pallas_call(functools.partial(layer_kernel, n, zs, ps, scale, grad_sca...]
where the time goes in v3:
time: 29.1 us; the launch traced here: 28.9 us
  Pallas kernels  28.3 us (97%)
  between operations  0.64 us (2%)
    pallas_call x1, Pallas kernels, shards(): pl.pallas_call(functools.partial(layer_kernel, n, zs, ps, scale, grad_sca...  27.5 us
    pallas_call x1, Pallas kernels, finish(): pl.pallas_call(finish_kernel, out_shape=tuple((jax.ShapeDtypeStruct(a.sha...  0.78 us

profile of v3, /device:TPU:0, one launch (start us, length us, event | category | flops | bytes accessed | tf_op | source)
XLA Modules:
  0.0 28.9 jit_solution(17453993230526338288)
XLA Ops:
  0.6 27.5 %layer.1 = (bf16[128,256]{1,0:T(8,128)(2,1)S(1)}, f32[128,128]{1,0:T(8,128)S(1)}, f32[128,256]{1,0:T(8,128)S(1)}, f32[128,256]{1,0:T(8,128)S(1)}) custom-call(s32[1,128]{1,0:T(1,128)} %bitcast.3, s32[1,128]{1,0:T(1,128)} %bitcast.4, s32[128,128,128]{2,1,0:T(8,128)} %counts.1, bf16[128,128]{1,0:T(8,128)(2,1)} %feat_h.1, s32[1,64]{1,0:T(1,128)} %bitcast.5, ...), custom_call_target="tpu_custom_call" | custom-call | tf_op jit(solution)/shard_map/layer/pallas_call | solution.py:342
  28.1 0.8 %finish.1 = (bf16[128,256]{1,0:T(8,128)(2,1)}, f32[128,128]{1,0:T(8,128)}, f32[128,256]{1,0:T(8,128)}, f32[128,256]{1,0:T(8,128)}) custom-call(bf16[128,256]{1,0:T(8,128)(2,1)S(1)} %get-tuple-element.8.refs_0_, f32[128,128]{1,0:T(8,128)S(1)} %get-tuple-element.9.refs_1_, f32[128,256]{1,0:T(8,128)S(1)} %get-tuple-element.10.refs_2_, ...), custom_call_target="tpu_custom_call" | custom-call | tf_op jit(solution)/shard_map/finish/pallas_call | solution.py:33

commit v4 on v3

--- a/solution.py
+++ b/solution.py
@@ -72,7 +72,9 @@
         return flip(mz, k) if paired else (mz + zs - k) % zs
 
     def prow(d):
-        return (mp + d) % ps
+        return flip(mp, d) if ps & (ps - 1) == 0 else (mp + d) % ps
+
+    outer = range(ps - 1, 0, -1)
 
     def send(src, dst, ssem, rsem, row, core):
         copy = pltpu.make_async_remote_copy(
@@ -117,7 +119,7 @@
                 barrier, inc=1, device_id=(mz * ps + prow(d), core), device_id_type=MESH
             )
     pl.semaphore_signal(barrier, inc=1, device_id=(me, other), device_id_type=MESH)
-    cube = range(1, ps) if zs > 1 else ()
+    cube = outer if zs > 1 else ()
     for d in cube:
         pl.semaphore_signal(
             barrier, inc=1, device_id=(zto(1) * ps + prow(d), rep), device_id_type=MESH
@@ -128,7 +130,7 @@
     pl.semaphore_wait(barrier, zs + 2 * (ps - 1) + len(cube))
 
     firsts = [zto(k) * ps + mp for k in [*range(2, zs), 1] if k < zs]
-    firsts += [mz * ps + prow(d) for d in range(1, ps)]
+    firsts += [mz * ps + prow(d) for d in outer]
     firsts += [zto(1) * ps + prow(d) for d in cube]
     relayed = max(zs - 2, 0)
     for k, row in enumerate(firsts):
@@ -191,7 +193,7 @@
     def pass_on(e):
         src = zfrom(e) * ps + mp
         arrived(gath.at[src], ag_z.at[zfrom(e)])
-        for d in range(1, ps):
+        for d in outer:
             send(
                 gath.at[src], gath.at[src], send_s.at[0], ag_r.at[zfrom(e)],
                 mz * ps + prow(d), rep,
@@ -234,7 +236,7 @@
     send(bt.at[rep], bt.at[rep], send_s.at[2], pair_r.at[1], me, other)
     wpart[0] = dot(feat[...], delta, TN).astype(jnp.bfloat16).reshape(wpart.shape[1:])
     wpart[1] = dot(neighbour, delta, TN).astype(jnp.bfloat16).reshape(wpart.shape[1:])
-    peers = [(mp, other)] + [(prow(d), core) for d in range(1, ps) for core in (rep, other)]
+    peers = [(mp, other)] + [(prow(d), core) for d in outer for core in (rep, other)]
     for p, core in peers:
         send(
             wpart.at[core, p], win.at[rep * ps + mp], send_s.at[3], late_r.at[0], mz * ps + p, core
@@ -250,7 +252,7 @@
         out = dot(back, plane_cols(zt))
         for j in range(ps):
             tt[zt * ps + j] = out[:, j * half : (j + 1) * half].astype(jnp.bfloat16)
-        for d in range(1, ps):
+        for d in outer:
             k = zt * (ps - 1) + d - 1
             send(
                 tt.at[zt * ps + prow(d)], r1.at[k], send_s.at[4],
@@ -264,7 +266,7 @@
     for p, core in peers:
         shard = shard + win[core * ps + p].astype(jnp.float32)
     wz[mz] = shard.astype(jnp.bfloat16)
-    for d in range(1, zs):
+    for d in range(zs - 1, 0, -1):
         send(wz.at[mz], wz.at[mz], send_s.at[5], late_r.at[1], zto(d) * ps + mp, rep)
 
     def plane_sum(zt):

time: 29.1 us -> 28.6 us (0.983)
  Pallas kernels: 28.3 us -> 27.8 us
    pallas_call x1, Pallas kernels: 27.5 us -> 27 us  [shards(): pl.pallas_call(functools.partial(layer_kernel, n, zs, ps, scale, grad_sca...]
where the time goes in v4:
time: 28.6 us; the launch traced here: 28.4 us
  Pallas kernels  27.8 us (97%)
  between operations  0.64 us (2%)
    pallas_call x1, Pallas kernels, shards(): pl.pallas_call(functools.partial(layer_kernel, n, zs, ps, scale, grad_sca...  27 us
    pallas_call x1, Pallas kernels, finish(): pl.pallas_call(finish_kernel, out_shape=tuple((jax.ShapeDtypeStruct(a.sha...  0.78 us

profile of v4, /device:TPU:0, one launch (start us, length us, event | category | flops | bytes accessed | tf_op | source)
XLA Modules:
  0.0 28.4 jit_solution(6830900324831133023)
XLA Ops:
  0.6 27.0 %layer.1 = (bf16[128,256]{1,0:T(8,128)(2,1)S(1)}, f32[128,128]{1,0:T(8,128)S(1)}, f32[128,256]{1,0:T(8,128)S(1)}, f32[128,256]{1,0:T(8,128)S(1)}) custom-call(s32[1,128]{1,0:T(1,128)} %bitcast.3, s32[1,128]{1,0:T(1,128)} %bitcast.4, s32[128,128,128]{2,1,0:T(8,128)} %counts.1, bf16[128,128]{1,0:T(8,128)(2,1)} %feat_h.1, s32[1,64]{1,0:T(1,128)} %bitcast.5, ...), custom_call_target="tpu_custom_call" | custom-call | tf_op jit(solution)/shard_map/layer/pallas_call | solution.py:344
  27.7 0.8 %finish.1 = (bf16[128,256]{1,0:T(8,128)(2,1)}, f32[128,128]{1,0:T(8,128)}, f32[128,256]{1,0:T(8,128)}, f32[128,256]{1,0:T(8,128)}) custom-call(bf16[128,256]{1,0:T(8,128)(2,1)S(1)} %get-tuple-element.8.refs_0_, f32[128,128]{1,0:T(8,128)S(1)} %get-tuple-element.9.refs_1_, f32[128,256]{1,0:T(8,128)S(1)} %get-tuple-element.10.refs_2_, ...), custom_call_target="tpu_custom_call" | custom-call | tf_op jit(solution)/shard_map/finish/pallas_call | solution.py:33
